TPU v7x, 512 devices: a whole 4x4x16 slice. The times are simulated.
512 devices in a mesh: row: 16 (over x, z_lo), col: 32 (over y, z_hi, core).
Axes of the slice: x: 4, y: 4, z: 16 (z_hi: 4, z_lo: 4; z = z_hi * 4 + z_lo), core: 2. Of those that a mesh axis runs over, the one named last changes fastest.
Arguments:
- features: bfloat16 [65536, 256], P(('col', 'row')), may hold values from -6 to 6
- weight: bfloat16 [256, 256], replicated, may hold values from -0.375 to 0.375
- cotangent: bfloat16 [65536, 256], P(('row', 'col')), may hold values from -6 to 6
- block_index: int32 [16, 32, 32], P('row', 'col'), may hold values from 0 to 511, as said below
- block_count: int32 [16, 32], P('row', 'col'), may hold values from 1 to 32, as said below
- block_values: bfloat16 [16, 32, 32, 128, 128], P('row', 'col'), may hold values from -0.125 to 0.125
Outputs:
- hidden_out: bfloat16 [65536, 256], P(('row', 'col'))
- input_grad: bfloat16 [65536, 256], P(('col', 'row'))
- weight_grad: float32 [256, 256], replicated
Inputs may be any that keep to these rules, and one draw needn't show every extreme that they name: `block_index`: the 32 entries of one tile are distinct; slots at or after the tile's count hold blocks that are not used. `block_count`: at least one tile holds exactly 32 blocks.
All inputs are finite; a program needn't handle non-finite values.
Results may differ from a plain program's by a relative error of at most 0.015.
Values may be sent and summed in bfloat16 or wider, within the bound.
A program may use at most 64 MiB of HBM per device.

v0:
```python
import math
import jax
import jax.numpy as jnp
from jax import lax
from jax.sharding import PartitionSpec as P

GROUP = 32


def forward_tile(blocks_in, values, index, count, rows_out):
    ncols = blocks_in.shape[0]
    size = blocks_in.shape[1]
    width = blocks_in.shape[2]
    lanes = jnp.arange(GROUP, dtype=jnp.int32)
    targets = jnp.arange(rows_out, dtype=jnp.int32)

    def forward_advance(group_id, totals):
        start = (group_id * GROUP).astype(jnp.int32)
        live = start + lanes < count
        picked = jnp.take(blocks_in, index % ncols, axis=0)
        product = jnp.einsum("gij,gjd->gid", values, picked, preferred_element_type=jnp.float32)
        selector = ((index // ncols)[None, :] == targets[:, None]) & live[None, :]
        return totals + jnp.einsum(
            "rg,gid->rid", selector.astype(jnp.float32), product, precision=lax.Precision.HIGHEST
        )

    zeros = jnp.zeros((rows_out, size, width), jnp.float32)
    groups = (count + GROUP - 1) // GROUP
    return lax.fori_loop(jnp.int32(0), groups, forward_advance, zeros)


def backward_tile(blocks_grad, values, index, count, cols_out):
    size = blocks_grad.shape[1]
    width = blocks_grad.shape[2]
    lanes = jnp.arange(GROUP, dtype=jnp.int32)
    targets = jnp.arange(cols_out, dtype=jnp.int32)

    def backward_advance(group_id, totals):
        start = (group_id * GROUP).astype(jnp.int32)
        live = start + lanes < count
        picked = jnp.take(blocks_grad, index // cols_out, axis=0)
        product = jnp.einsum("gij,gid->gjd", values, picked, preferred_element_type=jnp.float32)
        selector = ((index % cols_out)[None, :] == targets[:, None]) & live[None, :]
        return totals + jnp.einsum(
            "cg,gjd->cjd", selector.astype(jnp.float32), product, precision=lax.Precision.HIGHEST
        )

    zeros = jnp.zeros((cols_out, size, width), jnp.float32)
    groups = (count + GROUP - 1) // GROUP
    return lax.fori_loop(jnp.int32(0), groups, backward_advance, zeros)


def body(features, weight, cotangent, block_index, block_count, block_values):
    row_total = lax.axis_size("row")
    col_total = lax.axis_size("col")
    rows = features.shape[0]
    width = features.shape[1]
    size = block_values.shape[-1]
    block_rows = rows * col_total // size
    block_cols = rows * row_total // size
    index = block_index[0, 0]
    count = block_count[0, 0]
    values = block_values[0, 0]
    own_projected = jnp.dot(features, weight, preferred_element_type=jnp.float32).astype(
        jnp.bfloat16
    )
    projected = lax.all_gather(own_projected, "row", axis=0, tiled=True)
    partial_out = forward_tile(
        projected.reshape(block_cols, size, width), values, index, count, block_rows
    )
    summed_out = lax.psum_scatter(
        partial_out.reshape(block_rows * size, width).astype(jnp.bfloat16),
        "col",
        scatter_dimension=0,
        tiled=True,
    )
    grad_rows = lax.all_gather(cotangent, "col", axis=0, tiled=True)
    partial_back = backward_tile(
        grad_rows.reshape(block_rows, size, width), values, index, count, block_cols
    )
    partial_back = partial_back.reshape(block_cols * size, width)
    grad_sum = lax.psum_scatter(
        partial_back.astype(jnp.bfloat16), "row", scatter_dimension=0, tiled=True
    ).astype(jnp.float32)
    input_grad = jnp.dot(
        grad_sum, weight.astype(jnp.float32).T, precision=lax.Precision.HIGHEST
    ).astype(jnp.bfloat16)
    term = jnp.dot(features.astype(jnp.float32).T, grad_sum, precision=lax.Precision.HIGHEST)
    total = lax.psum(term, ("row", "col"))
    nodes = rows * row_total * col_total
    weight_grad = total / math.sqrt(nodes)
    return (summed_out, input_grad, weight_grad)


def solution(mesh):
    in_specs = (
        P(("col", "row"), None),
        P(),
        P(("row", "col"), None),
        P("row", "col", None),
        P("row", "col"),
        P("row", "col", None, None, None),
    )
    out_specs = (P(("row", "col"), None), P(("col", "row"), None), P())
    return jax.shard_map(body, mesh=mesh, in_specs=in_specs, out_specs=out_specs, check_vma=False)
```

profile of v0, /device:TPU:6, one launch (start us, length us, event | category | flops | bytes accessed | tf_op | source)
XLA Modules:
  0.0 881.2 jit_solution(7760522335443745997)
XLA Ops:
  7.2 0.7 all-gather.5.cloned.1.call-update
  8.6 0.7 fusion.42
  9.3 0.7 bitcast_sign_fusion.1
  10.0 84.2 %all-gather.5.cloned.1.call-done = bf16[4096,256]{1,0:T(8,128)(2,1)} async-done(((bf16[128,256]{1,0:T(8,128)(2,1)}), bf16[4096,256]{1,0:T(8,128)(2,1)}) %all-gather.5.cloned.1.call-update) | async-done | bytes 2097168 | tf_op jit(solution)/shard_map/all_gather | solution.py:77
  94.2 3.7 gather_fusion.1
  97.8 0.2 broadcast_in_dim.63
  98.1 0.4 copy-done.4
  98.5 15.7 %while.34 = (s32[]{:T(128)}, f32[16,128,256]{2,0,1:T(8,128)S(1)}, s32[]{:T(128)}, s32[32]{0:T(128)S(1)}, s32[32]{0:T(128)S(1)}, /*index=5*/s32[]{:T(128)}, s32[3...) while((s32[]{:T(128)}, f32[16,128,256]{2,0,1:T(8,128)S(1)}, ...), condition=%wide.region_4.5_spmd.clone, body=%wide.region_3.4_spmd.clone.sunk | while | flops 471336928 | bytes 24118400 | solution.py:50
  98.5 0.7 compare_and_fusion.4
  99.2 4.6 fusion.69
  103.8 5.5 copy.20
  109.3 4.8 fusion.70
  114.2 2.1 copy.17
  116.4 0.8 convolution_convert_fusion.1
  117.3 78.8 %reduce-scatter.5.cloned.1.call-done = bf16[128,256]{1,0:T(8,128)(2,1)} async-done(((bf16[2048,256]{1,0:T(8,128)(2,1)}), bf16[128,256]{1,0:T(8,128)(2,1)}) %reduce-scatter.5.cloned.1.call-update) | async-done | bytes 65552 | tf_op jit(solution)/shard_map/reduce_scatter | solution.py:82
  196.1 1.8 convolution_bitcast_fusion
  197.9 85.1 %all-gather.3.cloned.1.call-done = bf16[2048,256]{1,0:T(8,128)(2,1)} async-done(((bf16[128,256]{1,0:T(8,128)(2,1)}), bf16[2048,256]{1,0:T(8,128)(2,1)}) %all-gather.3.cloned.1.call-update) | async-done | bytes 1048592 | tf_op jit(solution)/shard_map/all_gather | solution.py:67
  283.0 2.5 broadcast_in_dim.62
  285.5 18.6 %while.35 = (s32[]{:T(128)}, f32[32,128,256]{2,0,1:T(8,128)}, s32[]{:T(128)}, s32[1,32]{1,0:T(1,128)S(1)}, s32[32]{0:T(128)S(1)}, /*index=5*/s32[1,32]{1,0:T(1,1...) while((s32[]{:T(128)}, f32[32,128,256]{2,0,1:T(8,128)}, ...), condition=%wide.region_1.2_spmd.clone.clone, body=%wide.region_0.1_spmd.clone.clone.sunk | while | flops 673190272 | bytes 32511760 | solution.py:29
  285.5 0.7 compare_and_fusion.5
  286.2 0.7 gather_fusion
  286.9 4.0 fusion.76
  290.9 5.5 copy.21
  296.4 7.7 fusion.78
  304.1 2.5 convert_element_type.25
  306.6 2.5 copy.11
  309.2 0.8 copy-done.3
  310.0 0.8 convolution_convert_fusion
  310.8 441.0 %all-reduce.2.cloned.1.call-done = f32[256,256]{0,1:T(8,128)} async-done(((f32[256,256]{0,1:T(8,128)}), f32[256,256]{0,1:T(8,128)}) %all-reduce.2.cloned.1.call-update) | async-done | bytes 262160 | tf_op jit(solution)/shard_map/psum | solution.py:89
  751.8 1.0 broadcast_multiply_fusion
  752.8 0.8 copy.13
  753.6 121.0 %reduce-scatter.3.cloned.1.call-done = bf16[128,256]{1,0:T(8,128)(2,1)} async-done(((bf16[4096,256]{1,0:T(8,128)(2,1)}), bf16[128,256]{1,0:T(8,128)(2,1)}) %reduce-scatter.3.cloned.1.call-update) | async-done | bytes 65552 | tf_op jit(solution)/shard_map/reduce_scatter | solution.py:71
  (23 shorter events, 0.3 us)
Async XLA Ops:
  7.2 109.2 %copy-start = (bf16[256,256]{1,0:T(8,128)(2,1)S(1)}, bf16[256,256]{1,0:T(8,128)(2,1)}, u32[]{:S(2)}) copy-start(bf16[256,256]{1,0:T(8,128)(2,1)} %param.11) | copy-start | bytes 393220
  7.2 87.0 %all-gather.5.cloned.1.call-start = ((), (), s32[]{:S(2)}) async-start(), calls=%async_computation.4 | async-start | bytes 2162688 | tf_op jit(solution)/shard_map/all_gather | solution.py:77
  7.9 188.2 %reduce-scatter.5.cloned.1.call-start = ((), (), s32[]{:S(2)}) async-start(), calls=%async_computation.5 | async-start | bytes 1114112 | tf_op jit(solution)/shard_map/reduce_scatter | solution.py:82
  97.8 0.7 copy-start.4
  114.2 2.2 copy-start.2
  116.3 166.7 %all-gather.3.cloned.1.call-start = ((), (), s32[]{:S(2)}) async-start(), calls=%async_computation.2 | async-start | bytes 1114112 | tf_op jit(solution)/shard_map/all_gather | solution.py:67
  117.2 634.6 %all-reduce.2.cloned.1.call-start = ((), (), s32[]{:S(2)}) async-start(), calls=%async_computation.6 | async-start | bytes 524288 | tf_op jit(solution)/shard_map/psum | solution.py:89
  197.9 676.8 %reduce-scatter.3.cloned.1.call-start = ((), (), s32[]{:S(2)}) async-start(), calls=%async_computation.3 | async-start | bytes 2162688 | tf_op jit(solution)/shard_map/reduce_scatter | solution.py:71
  283.0 2.5 copy-start.1
  309.1 0.8 copy-start.3
Sparse Core Ops, SparseCore 0:
  11.1 82.9 all-gather.4
  116.4 79.6 reduce-scatter.4
  199.0 83.9 all-gather.2
  289.8 461.9 all-reduce.1
  756.6 117.9 reduce-scatter.2
where the time goes:
time: 882 us; the launch traced here: 881 us
  waiting for transfers between devices  811 us (92%)
  local copies, waits for them, and re-layouts  24.8 us (3%)
  matrix products  24.6 us (3%)
  between operations  14.5 us (2%)
    psum x1, waiting for transfers between devices, body(): total = lax.psum(term, ('row', 'col'))  441 us
    reduce_scatter x1, waiting for transfers between devices, body(): lax.psum_scatter(partial_out.reshape(block_rows * size, width).astype(jnp...  121 us
    all_gather x1, waiting for transfers between devices, body(): projected = lax.all_gather(own_projected, 'row', axis=0, tiled=True)  85.1 us
    all_gather x1, waiting for transfers between devices, body(): grad_rows = lax.all_gather(cotangent, 'col', axis=0, tiled=True)  84.2 us
    reduce_scatter x1, waiting for transfers between devices, body(): lax.psum_scatter(partial_back.astype(jnp.bfloat16), 'row', scatter_dimens...  78.8 us
  transfers between devices with their start and end apart: 5, of which 5 were waited for; matrix products, arithmetic and copies ran while one was open for 4% of the time, Pallas kernels for 0%

commit v1 on v0

--- a/solution.py
+++ b/solution.py
@@ -74,7 +74,10 @@
         scatter_dimension=0,
         tiled=True,
     )
-    grad_rows = lax.all_gather(cotangent, "col", axis=0, tiled=True)
+    peers = lax.axis_size("col")
+    blocks = jnp.stack([cotangent for _ in range(peers)])
+    blocks = lax.all_to_all(blocks, "col", split_axis=0, concat_axis=0)
+    grad_rows = jnp.concatenate(blocks, axis=0)
     partial_back = backward_tile(
         grad_rows.reshape(block_rows, size, width), values, index, count, block_cols
     )

time: 882 us -> 912 us (1.034)
  starting transfers between devices: 0.2 us -> 18.4 us
  waiting for transfers between devices: 811 us -> 823 us
    all_to_all x0 -> x1, waiting for transfers between devices: none -> 94.1 us  [body(): blocks = lax.all_to_all(blocks, 'col', split_axis=0, concat_axis=0)]
    all_gather x1 -> x0, waiting for transfers between devices: 84.2 us -> none  [body(): grad_rows = lax.all_gather(cotangent, 'col', axis=0, tiled=True)]
    all_to_all x0 -> x1, starting transfers between devices: none -> 18.2 us  [body(): blocks = lax.all_to_all(blocks, 'col', split_axis=0, concat_axis=0)]
  transfers between devices with their start and end apart: 5 -> 5, of which waited for: 5 -> 5; matrix products, arithmetic and copies ran while one was open for 4% -> 3% of each run, Pallas kernels for 0% -> 0%
where the time goes in v1:
time: 912 us; the launch traced here: 911 us
  waiting for transfers between devices  823 us (90%)
  local copies, waits for them, and re-layouts  25.2 us (3%)
  matrix products  24.6 us (3%)
  starting transfers between devices  18.4 us (2%)
  between operations  14.5 us (2%)
    psum x1, waiting for transfers between devices, body(): total = lax.psum(term, ('row', 'col'))  441 us
    reduce_scatter x1, waiting for transfers between devices, body(): lax.psum_scatter(partial_out.reshape(block_rows * size, width).astype(jnp...  121 us
    all_to_all x1, waiting for transfers between devices, body(): blocks = lax.all_to_all(blocks, 'col', split_axis=0, concat_axis=0)  94.1 us
    all_gather x1, waiting for transfers between devices, body(): projected = lax.all_gather(own_projected, 'row', axis=0, tiled=True)  85.1 us
    reduce_scatter x1, waiting for transfers between devices, body(): lax.psum_scatter(partial_back.astype(jnp.bfloat16), 'row', scatter_dimens...  81.9 us
    all_to_all x1, starting transfers between devices, body(): blocks = lax.all_to_all(blocks, 'col', split_axis=0, concat_axis=0)  18.2 us
  transfers between devices with their start and end apart: 5, of which 5 were waited for; matrix products, arithmetic and copies ran while one was open for 3% of the time, Pallas kernels for 0%

profile of v1, /device:TPU:6, one launch (start us, length us, event | category | flops | bytes accessed | tf_op | source)
XLA Modules:
  0.0 911.0 jit_solution(13227467694994287031)
XLA Ops:
  7.2 2.5 stack.2
  9.6 18.2 %all-to-all-start = ((bf16[32,128,256]{2,1,0:T(8,128)(2,1)}), bf16[32,128,256]{2,1,0:T(8,128)(2,1)S(1)}, u32[]{:S(2)}, u32[]{:S(2)}) async-start(bf16[32,128,256]{2,1,0:T(8,128)(2,1)} %stack.2), calls=%async_computation.1 | async-start | bytes 4194304 | tf_op jit(solution)/shard_map/all_to_all | solution.py:79
  28.7 94.1 %all-to-all-done = bf16[32,128,256]{2,1,0:T(8,128)(2,1)S(1)} async-done(((bf16[32,128,256]{2,1,0:T(8,128)(2,1)}), bf16[32,128,256]{2,1,0:T(8,128)(2,1)S(1)}, u32[]{:S(2)}, u32[]{:S(2)}) %all-to-all-start) | async-done | bytes 2097184 | tf_op jit(solution)/shard_map/all_to_all | solution.py:79
  122.8 2.1 gather_fusion.1
  124.8 0.2 broadcast_in_dim.63
  125.1 15.7 %while.34 = (s32[]{:T(128)}, f32[16,128,256]{2,0,1:T(8,128)S(1)}, s32[]{:T(128)}, s32[32]{0:T(128)S(1)}, s32[32]{0:T(128)S(1)}, /*index=5*/s32[]{:T(128)}, s32[3...) while((s32[]{:T(128)}, f32[16,128,256]{2,0,1:T(8,128)S(1)}, ...), condition=%wide.region_4.5_spmd.clone, body=%wide.region_3.4_spmd.clone.sunk | while | flops 471336928 | bytes 24118400 | solution.py:50
  125.1 0.7 compare_and_fusion.4
  125.8 4.6 fusion.69
  130.4 5.5 copy.20
  135.9 4.8 fusion.70
  140.8 2.1 copy.17
  142.9 0.0 all-gather.2.cloned.1.call-start
  143.0 0.8 convolution_convert_fusion.1
  143.8 0.0 all-reduce.2.cloned.1.call-start
  143.9 81.9 %reduce-scatter.5.cloned.1.call-done = bf16[128,256]{1,0:T(8,128)(2,1)} async-done(((bf16[2048,256]{1,0:T(8,128)(2,1)}), bf16[128,256]{1,0:T(8,128)(2,1)}) %reduce-scatter.5.cloned.1.call-update) | async-done | bytes 65552 | tf_op jit(solution)/shard_map/reduce_scatter | solution.py:85
  225.7 1.8 convolution_bitcast_fusion
  227.6 85.1 %all-gather.2.cloned.1.call-done = bf16[2048,256]{1,0:T(8,128)(2,1)} async-done(((bf16[128,256]{1,0:T(8,128)(2,1)}), bf16[2048,256]{1,0:T(8,128)(2,1)}) %all-gather.2.cloned.1.call-update) | async-done | bytes 1048592 | tf_op jit(solution)/shard_map/all_gather | solution.py:67
  312.7 2.5 broadcast_in_dim.62
  315.2 18.6 %while.35 = (s32[]{:T(128)}, f32[32,128,256]{2,0,1:T(8,128)}, s32[]{:T(128)}, s32[1,32]{1,0:T(1,128)S(1)}, s32[32]{0:T(128)S(1)}, /*index=5*/s32[1,32]{1,0:T(1,1...) while((s32[]{:T(128)}, f32[32,128,256]{2,0,1:T(8,128)}, ...), condition=%wide.region_1.2_spmd.clone.clone, body=%wide.region_0.1_spmd.clone.clone.sunk | while | flops 673190272 | bytes 32511760 | solution.py:29
  315.2 0.7 compare_and_fusion.5
  315.9 0.7 gather_fusion
  316.6 4.0 fusion.76
  320.6 5.5 copy.21
  326.1 7.7 fusion.78
  333.7 2.5 convert_element_type.25
  336.3 2.5 copy.11
  338.8 0.8 copy-done.3
  339.6 0.8 convolution_convert_fusion
  340.4 441.2 %all-reduce.2.cloned.1.call-done = f32[256,256]{0,1:T(8,128)} async-done(((f32[256,256]{0,1:T(8,128)}), f32[256,256]{0,1:T(8,128)}) %all-reduce.2.cloned.1.call-update) | async-done | bytes 262160 | tf_op jit(solution)/shard_map/psum | solution.py:92
  781.6 1.0 broadcast_multiply_fusion
  782.6 0.8 copy.13
  783.4 121.1 %reduce-scatter.3.cloned.1.call-done = bf16[128,256]{1,0:T(8,128)(2,1)} async-done(((bf16[4096,256]{1,0:T(8,128)(2,1)}), bf16[128,256]{1,0:T(8,128)(2,1)}) %reduce-scatter.3.cloned.1.call-update) | async-done | bytes 65552 | tf_op jit(solution)/shard_map/reduce_scatter | solution.py:71
  (23 shorter events, 0.2 us)
Async XLA Ops:
  7.2 135.8 %copy-start = (bf16[256,256]{1,0:T(8,128)(2,1)S(1)}, bf16[256,256]{1,0:T(8,128)(2,1)}, u32[]{:S(2)}) copy-start(bf16[256,256]{1,0:T(8,128)(2,1)} %param.11) | copy-start | bytes 393220
  9.6 19.0 %copy-start.4 = (s32[1,1,32]{2,1,0:T(1,128)S(1)}, s32[1,1,32]{2,1,0:T(1,128)}, u32[]{:S(2)}) copy-start(s32[1,1,32]{2,1,0:T(1,128)} %param.13) | copy-start | bytes 388
  9.6 113.1 %all-to-all-start = ((bf16[32,128,256]{2,1,0:T(8,128)(2,1)}), bf16[32,128,256]{2,1,0:T(8,128)(2,1)S(1)}, u32[]{:S(2)}, u32[]{:S(2)}) async-start(bf16[32,128,256]{2,1,0:T(8,128)(2,1)} %stack.2), calls=%async_computation.1 | async-start | bytes 4194304 | tf_op jit(solution)/shard_map/all_to_all | solution.py:79
  27.9 197.8 %reduce-scatter.5.cloned.1.call-start = ((), (), s32[]{:S(2)}) async-start(), calls=%async_computation.5 | async-start | bytes 1114112 | tf_op jit(solution)/shard_map/reduce_scatter | solution.py:85
  140.8 2.2 copy-start.2
  142.9 169.7 %all-gather.2.cloned.1.call-start = ((), (), s32[]{:S(2)}) async-start(), calls=%async_computation.3 | async-start | bytes 1114112 | tf_op jit(solution)/shard_map/all_gather | solution.py:67
  143.8 637.8 %all-reduce.2.cloned.1.call-start = ((), (), s32[]{:S(2)}) async-start(), calls=%async_computation.6 | async-start | bytes 524288 | tf_op jit(solution)/shard_map/psum | solution.py:92
  227.5 677.0 %reduce-scatter.3.cloned.1.call-start = ((), (), s32[]{:S(2)}) async-start(), calls=%async_computation.4 | async-start | bytes 2162688 | tf_op jit(solution)/shard_map/reduce_scatter | solution.py:71
  312.7 2.5 copy-start.1
  338.8 0.8 copy-start.3
Sparse Core Ops, SparseCore 0:
  143.0 82.6 reduce-scatter.4
  228.6 84.0 all-gather.1
  319.6 461.9 all-reduce.1
  786.4 118.0 reduce-scatter.2
